TPU v7x, 32 devices: a whole 2x2x4 slice. The times are simulated.
32 devices in a mesh: pb: 8 (over z, x), ta: 4 (over y, core).
Axes of the slice: x: 2, y: 2, z: 4, core: 2. Of those that a mesh axis runs over, the one named last changes fastest.
Arguments:
- feat_one: bfloat16 [16, 256, 128], P('pb'), may hold values from -7 to 7
- feat_two: bfloat16 [4, 2048, 128], P('ta', 'pb'), may hold values from -7 to 7
- cot_flow: float32 [2, 16, 256], P(None, 'pb'), may hold values from -6 to 6
- enc_input: bfloat16 [16, 128, 256], P('pb', 'ta'), may hold values from -0.59765625 to 0.59765625
- enc_weight: bfloat16 [3, 3, 128, 128], P(None, None, 'ta'), may hold values from -0.1875 to 0.1875
Outputs:
- grad_two: float32 [4, 2048, 128], P('ta', 'pb')
- grad_input: float32 [16, 128, 256], P('pb', 'ta')
- grad_weight: float32 [3, 3, 128, 128], P(None, None, 'ta')
All inputs are finite; a program needn't handle non-finite values.
Results may differ from a plain program's by a relative error of at most 0.0047.
Values may be sent and summed in bfloat16 or wider, within the bound.
A program may use at most 64 MiB of HBM per device.

v0:
```python
import math

import jax
import jax.numpy as jnp
from jax import lax
from jax.sharding import PartitionSpec as P

FRAME_COLS = 512


def joined(part, axis, combine):
    gathered = jax.tree.map(lambda a: lax.all_gather(a, axis), part)

    def take(source):
        return jax.tree.map(lambda a: lax.dynamic_index_in_dim(a, source, 0, False), gathered)

    return lax.fori_loop(
        1, lax.axis_size(axis), lambda source, state: combine(state, take(source)), take(0)
    )


def padded_2(value, sides, width):
    for axis, dim in sides:
        size, length = (lax.axis_size(axis), value.shape[dim])
        up = [(i, (i + 1) % size) for i in range(size - 1)]
        down = [(j, i) for i, j in up]
        last = lax.slice_in_dim(value, length - width, length, axis=dim)
        first = lax.slice_in_dim(value, 0, width, axis=dim)
        before = lax.ppermute(last, axis, up)
        after = lax.ppermute(first, axis, down)
        value = jnp.concatenate([before, value, after], axis=dim)
    return value


def positions(offset, number):
    target_ids = offset + jnp.arange(number, dtype=jnp.int32)
    col_pos = (target_ids % FRAME_COLS).astype(jnp.float32) - FRAME_COLS / 2
    row_pos = (target_ids // FRAME_COLS).astype(jnp.float32)
    return (col_pos, row_pos)


def score_matrix(left, right, inv_scale):
    return (
        lax.dot_general(left, right, (((1,), (1,)), ((), ())), preferred_element_type=jnp.float32)
        * inv_scale
    )


def pull_matrix(flow_rows, offset, number):
    col_pos, row_pos = positions(offset, number)
    return flow_rows[0][:, None] * col_pos[None, :] + flow_rows[1][:, None] * row_pos[None, :]


def grad_scores(scores, pull, peak, total, mean_pull, inv_scale):
    prob = jnp.exp(scores - peak[:, None]) / total[:, None]
    return (prob * (pull - mean_pull[:, None]) * inv_scale).astype(jnp.bfloat16)


def merge_stats(first_set, second_set):
    peak = jnp.maximum(first_set[0], second_set[0])
    decay_one = jnp.exp(first_set[0] - peak)
    decay_two = jnp.exp(second_set[0] - peak)
    total = first_set[1] * decay_one + second_set[1] * decay_two
    weighted = first_set[2] * decay_one + second_set[2] * decay_two
    return (peak, total, weighted)


def per_device(feat_one, feat_two, cot_flow, enc_input, enc_weight):
    rows_dev, columns, channels = feat_one.shape
    num_queries = rows_dev * columns
    queries = feat_one.reshape(num_queries, channels)
    flow_rows = cot_flow.reshape(2, num_queries)
    inv_scale = 1.0 / math.sqrt(channels)
    tgt_dev = feat_two.shape[1]
    group_size = tgt_dev * lax.axis_size("pb")
    group_first = lax.axis_index("ta") * group_size
    targets = lax.all_gather(feat_two, "pb", axis=1, tiled=True)[0]
    block_rows = 2048
    while group_size % block_rows:
        block_rows = block_rows // 2
    nblocks = group_size // block_rows

    def block_terms(block_index):
        offset = block_index * block_rows
        target_block = lax.dynamic_slice_in_dim(targets, offset, block_rows, 0)
        scores = score_matrix(queries, target_block, inv_scale)
        pull = pull_matrix(flow_rows, group_first + offset, block_rows)
        return (target_block, scores, pull)

    def stat_step(block_index, running):
        peak, total, weighted = running
        target_block, scores, pull = block_terms(block_index)
        new_peak = jnp.maximum(peak, jnp.max(scores, axis=1))
        decay = jnp.exp(peak - new_peak)
        expo = jnp.exp(scores - new_peak[:, None])
        return (
            new_peak,
            total * decay + jnp.sum(expo, axis=1),
            weighted * decay + jnp.sum(expo * pull, axis=1),
        )

    start_stats = (
        jnp.full((num_queries,), -jnp.inf, jnp.float32),
        jnp.zeros((num_queries,), jnp.float32),
        jnp.zeros((num_queries,), jnp.float32),
    )
    local_stats = lax.fori_loop(0, nblocks, stat_step, start_stats)
    peak, total, weighted = joined(local_stats, "ta", merge_stats)
    mean_pull = weighted / total
    zero_query = jnp.zeros((num_queries, channels), jnp.float32)

    def both_step(block_index, carry):
        accum, target_terms = carry
        target_block, scores, pull = block_terms(block_index)
        score_grad = grad_scores(scores, pull, peak, total, mean_pull, inv_scale)
        accum = accum + jnp.dot(score_grad, target_block, preferred_element_type=jnp.float32)
        term = lax.dot_general(
            score_grad, queries, (((0,), (0,)), ((), ())), preferred_element_type=jnp.float32
        )
        target_terms = lax.dynamic_update_slice_in_dim(
            target_terms, term, block_index * block_rows, 0
        )
        return (accum, target_terms)

    partial_grad, target_terms = lax.fori_loop(
        0, nblocks, both_step, (zero_query, jnp.zeros((group_size, channels), jnp.float32))
    )
    grad_two = lax.psum_scatter(target_terms, "pb", scatter_dimension=0, tiled=True)
    feat_grad = lax.psum(partial_grad, "ta").astype(jnp.bfloat16)
    grad_two = grad_two.reshape(1, tgt_dev, channels)
    padded = padded_2(feat_grad.reshape(rows_dev, columns, channels), (("pb", 0),), 1)
    padded = jnp.pad(padded, ((0, 0), (1, 1), (0, 0)))
    cin_dev = enc_input.shape[1]
    grad_input = jnp.zeros((rows_dev, cin_dev, columns), jnp.float32)
    weight_parts = []
    for row_off in range(3):
        for col_off in range(3):
            shifted = padded[
                2 - row_off : 2 - row_off + rows_dev, 2 - col_off : 2 - col_off + columns
            ]
            grad_input = grad_input + jnp.einsum(
                "yxo,io->yix",
                shifted,
                enc_weight[row_off, col_off],
                preferred_element_type=jnp.float32,
            )
            weight_parts.append(
                jnp.einsum("yix,yxo->io", enc_input, shifted, preferred_element_type=jnp.float32)
            )
    grad_weight = jnp.stack(weight_parts).reshape(3, 3, cin_dev, channels)
    grad_weight = lax.psum(grad_weight, "pb")
    return (grad_two, grad_input, grad_weight)


def solution(mesh):
    in_specs = (
        P("pb", None, None),
        P("ta", "pb", None),
        P(None, "pb", None),
        P("pb", "ta", None),
        P(None, None, "ta", None),
    )
    out_specs = (P("ta", "pb", None), P("pb", "ta", None), P(None, None, "ta", None))
    return jax.shard_map(
        per_device, mesh=mesh, in_specs=in_specs, out_specs=out_specs, check_vma=False
    )
```

profile of v0, /device:TPU:0, one launch (start us, length us, event | category | flops | bytes accessed | tf_op | source)
XLA Modules:
  0.0 237.9 jit_solution(1347143412521580529)
XLA Ops:
  7.2 0.0 copy-start
  7.2 0.0 all-reduce.4.cloned.1.call-start
  7.3 0.7 slice_bitcast_fusion.3
  8.0 33.2 %all_gather.17 = bf16[1,2048,128]{2,1,0:T(8,128)(2,1)S(1)} all-gather(bf16[1,256,128]{2,1,0:T(8,128)(2,1)} %param.8), channel_id=1, replica_groups=mesh['pb'=8,'ta'=4] {'pb'}, dimensions={1}, use_global_device_ids=true | all-gather | bytes 589824 | tf_op jit(solution)/shard_map/all_gather | solution.py:77
  41.2 0.0 copy-done
  41.2 0.8 multiply_reduce_fusion.1
  42.0 0.0 copy-start.1
  42.0 1.9 copy-done.1
  44.0 1.9 multiply_reduce_fusion
  45.8 5.2 %all-gather.2 = f32[4,1,512]{2,1,0:T(1,128)S(1)} all-gather(f32[1,1,512]{2,1,0:T(1,128)S(1)} %bitcast.205), channel_id=1, replica_groups=mesh['pb'=8,'ta'=4] {'ta'}, dimensions={0}, use_global_device_ids=true | all-gather | bytes 10240 | tf_op jit(solution)/shard_map/all_gather | solution.py:12
  51.0 5.2 %all-gather.3 = f32[4,1,512]{2,1,0:T(1,128)S(1)} all-gather(f32[1,1,512]{2,1,0:T(1,128)S(1)} %bitcast.204), channel_id=1, replica_groups=mesh['pb'=8,'ta'=4] {'ta'}, dimensions={0}, use_global_device_ids=true | all-gather | bytes 10240 | tf_op jit(solution)/shard_map/all_gather | solution.py:12
  56.2 5.2 %all-gather.1 = f32[4,1,512]{2,1,0:T(1,128)S(1)} all-gather(f32[1,1,512]{2,1,0:T(1,128)S(1)} %bitcast.199), channel_id=2, replica_groups=mesh['pb'=8,'ta'=4] {'ta'}, dimensions={0}, use_global_device_ids=true | all-gather | bytes 10240 | tf_op jit(solution)/shard_map/all_gather | solution.py:12
  61.4 0.3 while.12
  61.7 0.0 copy-start.2
  61.7 3.5 %multiply_convert_fusion = bf16[512,2048]{1,0:T(8,128)(2,1)S(1)} fusion(f32[512,2048]{1,0:T(8,128)} %copy-done.1, f32[512]{0:T(512)S(1)} %div.37, f32[512]{0:T(512)S(1)} %get-tuple-element.242, f32[512]{0:T(512)S(1)} %get-tuple-element.241, f32[2048]{0:T(1024)S(1)} %fusion.50, f32[512]{0:T(512)S(1)} %bitcast.203, f32[2048]{0:T(1024)S(1)} %fusion.49, ...), kind=kLoop, calls=%fused_computation.7 | loop fusion | flops 10485760 | bytes 6318080 | tf_op jit(solution)/shard_map/while/body/eval_jaxpr/convert_element_type | solution.py:56
  65.2 0.7 fusion.13
  66.0 14.5 %all-reduce.5 = bf16[512,128]{1,0:T(8,128)(2,1)S(1)} all-reduce(f32[512,128]{1,0:T(8,128)S(1)} %fusion.13), channel_id=1, replica_groups=mesh['pb'=8,'ta'=4] {'ta'}, use_global_device_ids=true, to_apply=%region_6.7 | all-reduce | flops 65536 | bytes 393216 | tf_op jit(solution)/shard_map/psum | solution.py:129
  80.5 3.6 %collective-permute-start = (bf16[1,256,128]{2,1,0:T(8,128)(2,1)S(1)}, bf16[1,256,128]{2,1,0:T(8,128)(2,1)S(1)}, u32[]{:S(2)}, u32[]{:S(2)}) collective-permute-start(bf16[1,256,128]{2,1,0:T(8,128)(2,1)S(1)} %get-tuple-element.264), channel_id=1, source_target_pairs={{0,4},{4,8},{8,12},{12,16},{16,20},{20,24},{24,28},{1,5},{5,9},{9,... | collective-permute-start | bytes 196616 | tf_op jit(solution)/shard_map/ppermute | solution.py:29
  84.1 1.3 collective-permute-start.1
  85.4 0.6 collective-permute-done
  86.0 4.3 %collective-permute-done.1 = bf16[1,256,128]{2,1,0:T(8,128)(2,1)S(1)} collective-permute-done((bf16[1,256,128]{2,1,0:T(8,128)(2,1)S(1)}, bf16[1,256,128]{2,1,0:T(8,128)(2,1)S(1)}, u32[]{:S(2)}, u32[]{:S(2)}) %collective-permute-start.1) | collective-permute-done | bytes 65568 | tf_op jit(solution)/shard_map/ppermute | solution.py:30
  90.3 0.1 fusion.21
  90.3 0.0 copy-done.2
  90.4 0.2 fusion.11
  90.5 0.1 fusion.10
  90.6 0.1 fusion.9
  90.8 0.2 fusion.8
  90.9 0.0 copy-start.4
  91.0 0.1 fusion.7
  91.1 0.1 fusion.6
  91.2 0.2 fusion.5
  91.4 0.1 fusion.4
  91.5 0.1 fusion.3
  91.7 0.0 copy-start.3
  91.7 0.7 copy-done.3
  92.3 0.0 all-reduce.4.cloned.1.call-update
  92.4 0.0 reduce-scatter.2.cloned.1.call-start
  92.4 1.7 fusion.80
  94.1 0.0 reduce-scatter.2.cloned.1.call-update
  94.1 0.0 copy-done.4
  94.2 0.1 fusion.22
  94.3 0.2 fusion.36
  94.5 0.2 convolution_add_fusion.6
  94.6 0.1 convolution_add_fusion.5
  94.8 0.2 convolution_add_fusion.4
  94.9 0.1 convolution_add_fusion.3
  95.1 0.2 convolution_add_fusion.2
  95.2 0.2 convolution_add_fusion.1
  95.4 0.8 fusion.2
  96.2 66.0 %all-reduce.4.cloned.1.call-done = f32[3,3,32,128]{3,2,1,0:T(8,128)} async-done(((f32[3,3,32,128]{3,2,1,0:T(8,128)}), f32[3,3,32,128]{3,2,1,0:T(8,128)}) %all-reduce.4.cloned.1.call-update) | async-done | bytes 147472 | tf_op jit(solution)/shard_map/psum | solution.py:151
  162.3 67.2 %reduce-scatter.2.cloned.1.call-done = f32[256,128]{1,0:T(8,128)} async-done(((f32[2048,128]{1,0:T(8,128)}), f32[256,128]{1,0:T(8,128)}) %reduce-scatter.2.cloned.1.call-update) | async-done | bytes 131088 | tf_op jit(solution)/shard_map/reduce_scatter | solution.py:128
  229.5 1.6 copy.42
  (28 shorter events, 0.2 us)
Async XLA Ops:
  7.2 34.1 %copy-start = (bf16[2,256,128]{2,1,0:T(8,128)(2,1)S(1)}, bf16[2,256,128]{2,1,0:T(8,128)(2,1)}, u32[]{:S(2)}) copy-start(bf16[2,256,128]{2,1,0:T(8,128)(2,1)} %param.7) | copy-start | bytes 393220
  7.2 155.1 %all-reduce.4.cloned.1.call-start = ((), (), s32[]{:S(2)}) async-start(), calls=%async_computation.2 | async-start | bytes 294912 | tf_op jit(solution)/shard_map/psum | solution.py:151
  42.0 1.9 copy-start.1
  61.7 28.6 %copy-start.2 = (bf16[2,32,256]{2,1,0:T(8,128)(2,1)S(1)}, bf16[2,32,256]{2,1,0:T(8,128)(2,1)}, u32[]{:S(2)}) copy-start(bf16[2,32,256]{2,1,0:T(8,128)(2,1)} %param.10) | copy-start | bytes 98308
  80.5 5.5 %collective-permute-start = (bf16[1,256,128]{2,1,0:T(8,128)(2,1)S(1)}, bf16[1,256,128]{2,1,0:T(8,128)(2,1)S(1)}, u32[]{:S(2)}, u32[]{:S(2)}) collective-permute-start(bf16[1,256,128]{2,1,0:T(8,128)(2,1)S(1)} %get-tuple-element.264), channel_id=1, source_target_pairs={{0,4},{4,8},{8,12},{12,16},{16,20},{20,24},{24,28},{1,5},{5,9},{9,... | collective-permute-start | bytes 196616 | tf_op jit(solution)/shard_map/ppermute | solution.py:29
  84.1 6.2 %collective-permute-start.1 = (bf16[1,256,128]{2,1,0:T(8,128)(2,1)S(1)}, bf16[1,256,128]{2,1,0:T(8,128)(2,1)S(1)}, u32[]{:S(2)}, u32[]{:S(2)}) collective-permute-start(bf16[1,256,128]{2,1,0:T(8,128)(2,1)S(1)} %get-tuple-element.265), channel_id=1, source_target_pairs={{4,0},{8,4},{12,8},{16,12},{20,16},{24,20},{28,24},{5,1},{9,5},{13... | collective-permute-start | bytes 196616 | tf_op jit(solution)/shard_map/ppermute | solution.py:30
  90.9 3.2 %copy-start.4 = (bf16[3,3,32,128]{3,2,1,0:T(8,128)(2,1)S(1)}, bf16[3,3,32,128]{3,2,1,0:T(8,128)(2,1)}, u32[]{:S(2)}) copy-start(bf16[3,3,32,128]{3,2,1,0:T(8,128)(2,1)} %param.11) | copy-start | bytes 221188
  91.7 0.7 copy-start.3
  92.4 137.1 %reduce-scatter.2.cloned.1.call-start = ((), (), s32[]{:S(2)}) async-start(), calls=%async_computation.1 | async-start | bytes 1179648 | tf_op jit(solution)/shard_map/reduce_scatter | solution.py:128
Sparse Core Ops, SparseCore 0:
  92.5 69.7 all-reduce.3
  166.2 63.1 reduce-scatter.1
where the time goes:
time: 238 us
  waiting for transfers between devices  138 us (58%)
  blocking collectives  63.3 us (27%)
  between operations  14.2 us (6%)
  matrix products  6.56 us (3%)
  other arithmetic  5.61 us (2%)
  local copies, waits for them, and re-layouts  5 us (2%)
  starting transfers between devices  4.93 us (2%)
    reduce_scatter x1, waiting for transfers between devices, per_device(): lax.psum_scatter(target_terms, 'pb', scatter_dimension=0, tiled=True)  67.2 us
    psum x1, waiting for transfers between devices, per_device(): grad_weight = lax.psum(grad_weight, 'pb')  66 us
    all_gather x1, blocking collectives, per_device(): targets = lax.all_gather(feat_two, 'pb', axis=1, tiled=True)[0]  33.2 us
    all_gather x3, blocking collectives, joined(): gathered = jax.tree.map(lambda a: lax.all_gather(a, axis), part)  15.5 us
    psum x1, blocking collectives, per_device(): feat_grad = lax.psum(partial_grad, 'ta').astype(jnp.bfloat16)  14.5 us
    unnamed x17, local copies, waits for them, and re-layouts  4.92 us
  transfers between devices with their start and end apart: 4, of which 4 were waited for; matrix products, arithmetic and copies ran while one was open for 2% of the time, Pallas kernels for 0%

commit v1 on v0

v1 whole, which is shorter than its diff:
```python
import functools
import math

import jax
import jax.numpy as jnp
from jax import lax
from jax.experimental import pallas as pl
from jax.experimental.pallas import tpu as pltpu
from jax.sharding import PartitionSpec as P

FRAME_COLS = 512
MESH = pl.DeviceIdType.MESH
F32 = jnp.float32
BF16 = jnp.bfloat16


def remote(src, dst, send_sem, recv_sem, where):
    return pltpu.make_async_remote_copy(
        src_ref=src,
        dst_ref=dst,
        send_sem=send_sem,
        recv_sem=recv_sem,
        device_id=where,
        device_id_type=MESH,
    )


def matmul(left, right, dims):
    return lax.dot_general(left, right, (dims, ((), ())), preferred_element_type=F32)


def moved(value, step):
    if step == 0:
        return value
    width = value.shape[1]
    lane = lax.broadcasted_iota(jnp.int32, value.shape, 1)
    rolled = pltpu.roll(value, step % width, 1)
    edge = 0 if step > 0 else width - 1
    return jnp.where(lane == edge, 0.0, rolled)


def kernel(
    n_pb, n_ta, rows, cols, gw_rows,
    q_ref, k_ref, flow_ref, in_ref, w_ref,
    g2_ref, gi_ref, gw_ref,
    k_all, expo, iota, peaks, totals, pulls, stats, stats_in,
    g_out, g_in, f_part, f_in, f_all, halo_in, in_sh, z_buf,
    edge_out, edge_in, gw_part, gw_send, gw_in, gw_all,
    kz_send, kx_send, k_recv, s_send, s_recv, g_send, g_recv,
    f_send, f_recv, a_send, a_recv, h_send, h_recv, e_send, e_recv,
    w_send, w_recv, v_send, v_recv,
):
    me = lax.axis_index("pb")
    grp = lax.axis_index("ta")
    zz, xx = me // 2, me % 2
    n_z = n_pb // 2
    mate = zz * 2 + (1 - xx)
    n_q, chan = q_ref.shape
    tgt = k_ref.shape[0]
    n_own = gw_part.shape[0] // gw_rows
    inv_scale = 1.0 / math.sqrt(chan)
    unit = inv_scale / math.log(2.0)

    barrier = pltpu.get_barrier_semaphore()

    def greet(d, _):
        pl.semaphore_signal(
            barrier, inc=1, device_id={"pb": lax.rem(me + d, n_pb)}, device_id_type=MESH
        )
        return 0

    lax.fori_loop(1, n_pb, greet, 0)
    for d in range(1, n_ta):
        pl.semaphore_signal(
            barrier, inc=1, device_id={"ta": lax.rem(grp + d, n_ta)}, device_id_type=MESH
        )
    k_all[me] = k_ref[...]
    iota[...] = lax.broadcasted_iota(jnp.int32, (tgt, n_q), 0).astype(F32)
    pl.semaphore_wait(barrier, n_pb - 1 + n_ta - 1)

    def z_copy(d):
        to = lax.rem(zz + d, n_z)
        return remote(
            k_ref, k_all.at[me], kz_send.at[d], k_recv.at[me], {"pb": to * 2 + xx}
        )

    def x_copy(d):
        origin = lax.rem(zz + n_z - d, n_z) * 2 + xx
        return remote(
            k_all.at[origin], k_all.at[origin], kx_send.at[d], k_recv.at[origin], {"pb": mate}
        )

    own_copy = remote(k_ref, k_all.at[me], kx_send.at[0], k_recv.at[me], {"pb": mate})
    own_copy.start()
    for d in range(1, n_z):
        z_copy(d).start()

    up = {"pb": lax.rem(me + 1, n_pb)}
    down = {"pb": lax.rem(me + n_pb - 1, n_pb)}
    h_up = remote(in_ref.at[rows - 1], halo_in.at[0], h_send.at[0], h_recv.at[0], up)
    h_down = remote(in_ref.at[0], halo_in.at[1], h_send.at[1], h_recv.at[1], down)
    h_up.start()
    h_down.start()

    def score_block(origin):
        raw = matmul(k_all[origin], q_ref[...], ((1,), (1,)))
        peak = jnp.max(raw, axis=0, keepdims=True) * unit
        value = jnp.exp2(raw * unit - peak)
        expo[origin] = value
        k0 = (grp * n_pb + origin) * tgt
        col0 = (lax.rem(k0, FRAME_COLS) - FRAME_COLS // 2).astype(F32)
        row = (k0 // FRAME_COLS).astype(F32)
        total = jnp.sum(value, axis=0, keepdims=True)
        along = jnp.sum(value * iota[...], axis=0, keepdims=True)
        peaks[origin] = peak
        totals[origin] = total
        pulls[origin] = flow_ref[0:1, :] * (along + col0 * total) + flow_ref[1:2, :] * (
            row * total
        )

    score_block(me)
    for y in range(rows):
        value = in_ref[y].astype(F32)
        cin = value.shape[0]
        for b in range(3):
            in_sh[b * cin : (b + 1) * cin, (y + 1) * cols : (y + 2) * cols] = moved(
                value, 1 - b
            ).astype(BF16)

    def arrived(origin):
        remote(
            k_all.at[origin], k_all.at[origin], kx_send.at[0], k_recv.at[origin], {"pb": mate}
        ).wait_recv()

    arrived(mate)
    score_block(mate)

    def z_step(d, _):
        origin = lax.rem(zz + n_z - d, n_z) * 2 + xx
        arrived(origin)
        x_copy(d).start()
        score_block(origin)
        return 0

    lax.fori_loop(1, n_z, z_step, 0)

    def x_step(d, _):
        origin = lax.rem(zz + n_z - d, n_z) * 2 + (1 - xx)
        arrived(origin)
        score_block(origin)
        return 0

    lax.fori_loop(1, n_z, x_step, 0)

    all_peaks = peaks[...]
    peak = jnp.max(all_peaks, axis=0)
    decay = jnp.exp2(all_peaks - peak[None])
    stats[0:1, :] = peak
    stats[1:2, :] = jnp.sum(totals[...] * decay, axis=0)
    stats[2:3, :] = jnp.sum(pulls[...] * decay, axis=0)
    stat_copies = []
    for d in range(1, n_ta):
        stat_copies.append(
            remote(
                stats,
                stats_in.at[grp],
                s_send.at[d],
                s_recv.at[grp],
                {"ta": lax.rem(grp + d, n_ta)},
            )
        )
        stat_copies[-1].start()

    h_up.wait_recv()
    h_down.wait_recv()
    for side, place in ((0, 0), (1, rows + 1)):
        value = halo_in[side].astype(F32)
        at_end = (me == 0) if side == 0 else (me == n_pb - 1)
        value = value * jnp.where(at_end, 0.0, 1.0)
        for b in range(3):
            in_sh[b * cin : (b + 1) * cin, place * cols : (place + 1) * cols] = moved(
                value, 1 - b
            ).astype(BF16)

    run = (stats[0:1, :], stats[1:2, :], stats[2:3, :])
    for d in range(1, n_ta):
        frm = lax.rem(grp + n_ta - d, n_ta)
        remote(
            stats, stats_in.at[frm], s_send.at[d], s_recv.at[frm], {"ta": frm}
        ).wait_recv()
        other = stats_in[frm]
        top = jnp.maximum(run[0], other[0:1, :])
        one = jnp.exp2(run[0] - top)
        two = jnp.exp2(other[0:1, :] - top)
        run = (
            top,
            run[1] * one + other[1:2, :] * two,
            run[2] * one + other[2:3, :] * two,
        )
    peak, total, weighted = run
    mean = weighted / total
    weight = inv_scale / total
    stats_in[grp, 0:1, :] = peak
    stats_in[grp, 1:2, :] = mean
    stats_in[grp, 2:3, :] = weight
    f_part[...] = jnp.zeros_like(f_part)

    def grad_block(origin):
        k0 = (grp * n_pb + origin) * tgt
        col0 = (lax.rem(k0, FRAME_COLS) - FRAME_COLS // 2).astype(F32)
        row = (k0 // FRAME_COLS).astype(F32)
        scale = jnp.exp2(peaks[origin] - stats_in[grp, 0:1, :]) * stats_in[grp, 2:3, :]
        slope = flow_ref[0:1, :]
        rest = col0 * slope + row * flow_ref[1:2, :] - stats_in[grp, 1:2, :]
        grad = (expo[origin] * scale * (iota[...] * slope + rest)).astype(BF16)
        f_part[...] += matmul(k_all[origin], grad, ((0,), (0,)))
        return matmul(grad, q_ref[...], ((1,), (0,)))

    def g_copy(d):
        to = lax.rem(me + d, n_pb)
        return remote(g_out.at[to], g_in.at[me], g_send.at[d], g_recv.at[me], {"pb": to})

    def grad_step(d, _):
        to = lax.rem(me + d, n_pb)
        g_out[to] = grad_block(to).astype(BF16)
        g_copy(d).start()
        return 0

    lax.fori_loop(1, n_pb, grad_step, 0)
    g2_ref[...] = grad_block(me)

    part = chan // n_ta

    def rows_of(ref, index):
        return ref.at[pl.ds(pl.multiple_of(index * part, part), part), :]

    f_all[...] = f_part[...].astype(BF16)
    f_copies = []
    for d in range(1, n_ta):
        to = lax.rem(grp + d, n_ta)
        f_copies.append(
            remote(rows_of(f_all, to), f_in.at[grp], f_send.at[d], f_recv.at[grp], {"ta": to})
        )
        f_copies[-1].start()
    total_f = f_part[pl.ds(pl.multiple_of(grp * part, part), part), :]
    for d in range(1, n_ta):
        frm = lax.rem(grp + n_ta - d, n_ta)
        remote(
            f_in.at[frm], f_in.at[frm], f_send.at[d], f_recv.at[frm], {"ta": frm}
        ).wait_recv()
        total_f = total_f + f_in[frm].astype(F32)
    for copy in f_copies:
        copy.wait_send()
    z_buf[pl.ds(pl.multiple_of(grp * part, part), part), :] = total_f.astype(BF16)
    a_copies = []
    for d in range(1, n_ta):
        to = lax.rem(grp + d, n_ta)
        a_copies.append(
            remote(
                rows_of(z_buf, grp), rows_of(z_buf, grp), a_send.at[d], a_recv.at[grp], {"ta": to}
            )
        )
        a_copies[-1].start()
    for d in range(1, n_ta):
        frm = lax.rem(grp + n_ta - d, n_ta)
        remote(
            rows_of(z_buf, frm), rows_of(z_buf, frm), a_send.at[d], a_recv.at[frm], {"ta": frm}
        ).wait_recv()

    feat = z_buf[...]
    width = 3 * cin
    for a in range(3):
        gw_part[a * width : (a + 1) * width, :] = matmul(
            in_sh[:, a * cols : (a + rows) * cols], feat, ((1,), (1,))
        )
    gw_send[...] = gw_part[...].astype(BF16)

    def gw_chunk(ref, index):
        return ref.at[pl.ds(pl.multiple_of(index * gw_rows, gw_rows), gw_rows), :]

    def w_copy(d):
        to = lax.rem(me + d, n_pb)
        return to, remote(
            gw_chunk(gw_send, to), gw_in.at[me], w_send.at[d], w_recv.at[me], {"pb": to}
        )

    def w_start(d, _):
        to = lax.rem(me + d, n_pb)

        @pl.when(to < n_own)
        def _():
            w_copy(d)[1].start()

        return 0

    lax.fori_loop(1, n_pb, w_start, 0)

    spread = matmul(w_ref[...], feat, ((1,), (0,)))
    outs = [None] * (rows + 2)
    for r in range(rows):
        for a in range(3):
            term = None
            for b in range(3):
                first = (a * 3 + b) * cin
                piece = moved(
                    spread[first : first + cin, r * cols : (r + 1) * cols], b - 1
                )
                term = piece if term is None else term + piece
            place = r + a
            outs[place] = term if outs[place] is None else outs[place] + term
    edge_out[0] = outs[rows + 1]
    edge_out[1] = outs[0]
    e_up = remote(edge_out.at[0], edge_in.at[0], e_send.at[0], e_recv.at[0], up)
    e_down = remote(edge_out.at[1], edge_in.at[1], e_send.at[1], e_recv.at[1], down)
    e_up.start()
    e_down.start()
    for y in range(rows):
        gi_ref[y] = outs[y + 1]

    @pl.when(me < n_own)
    def _():
        first = pl.multiple_of(me * gw_rows, gw_rows)
        gw_all[pl.ds(first, gw_rows), :] = gw_part[pl.ds(first, gw_rows), :]

        def add(d, _):
            frm = lax.rem(me + n_pb - d, n_pb)
            remote(
                gw_in.at[frm], gw_in.at[frm], w_send.at[d], w_recv.at[frm], {"pb": frm}
            ).wait_recv()
            gw_all[pl.ds(first, gw_rows), :] += gw_in[frm].astype(F32)
            return 0

        lax.fori_loop(1, n_pb, add, 0)

        def give(d, _):
            to = lax.rem(me + d, n_pb)
            remote(
                gw_chunk(gw_all, me), gw_chunk(gw_all, me), v_send.at[d], v_recv.at[me],
                {"pb": to},
            ).start()
            return 0

        lax.fori_loop(1, n_pb, give, 0)

    def g_add(d, _):
        frm = lax.rem(me + n_pb - d, n_pb)
        remote(
            g_in.at[frm], g_in.at[frm], g_send.at[d], g_recv.at[frm], {"pb": frm}
        ).wait_recv()
        g2_ref[...] += g_in[frm].astype(F32)
        return 0

    lax.fori_loop(1, n_pb, g_add, 0)

    e_up.wait_recv()
    e_down.wait_recv()
    gi_ref[0] += edge_in[0] * jnp.where(me == 0, 0.0, 1.0)
    gi_ref[rows - 1] += edge_in[1] * jnp.where(me == n_pb - 1, 0.0, 1.0)

    def v_wait(d, _):
        frm = lax.rem(me + n_pb - d, n_pb)

        @pl.when(frm < n_own)
        def _():
            remote(
                gw_chunk(gw_all, frm), gw_chunk(gw_all, frm), v_send.at[d], v_recv.at[frm],
                {"pb": frm},
            ).wait_recv()

        return 0

    lax.fori_loop(1, n_pb, v_wait, 0)
    gw_ref[...] = gw_all[...]

    own_copy.wait_send()
    for d in range(1, n_z):
        z_copy(d).wait_send()
        x_copy(d).wait_send()
    for copy in (h_up, h_down, e_up, e_down, *stat_copies, *a_copies):
        copy.wait_send()

    def drain(d, _):
        g_copy(d).wait_send()

        @pl.when(lax.rem(me + d, n_pb) < n_own)
        def _():
            w_copy(d)[1].wait_send()

        @pl.when(me < n_own)
        def _():
            remote(
                gw_chunk(gw_all, me), gw_chunk(gw_all, me), v_send.at[d], v_recv.at[me],
                {"pb": lax.rem(me + d, n_pb)},
            ).wait_send()

        return 0

    lax.fori_loop(1, n_pb, drain, 0)


def per_device(n_pb, n_ta, feat_one, feat_two, cot_flow, enc_input, enc_weight):
    rows, cols, chan = feat_one.shape
    n_q = rows * cols
    tgt = feat_two.shape[1]
    cin = enc_input.shape[1]
    taps = 9 * cin
    assert n_pb % 2 == 0 and FRAME_COLS % tgt == 0 and taps % 16 == 0
    gw_rows = 16 * pl.cdiv(taps // 16, n_pb)
    assert taps % gw_rows == 0
    vmem = pl.BlockSpec(memory_space=pltpu.VMEM)
    dma = pltpu.SemaphoreType.DMA
    n_z = n_pb // 2
    outs = pl.pallas_call(
        functools.partial(kernel, n_pb, n_ta, rows, cols, gw_rows),
        out_shape=(
            jax.ShapeDtypeStruct((tgt, chan), F32),
            jax.ShapeDtypeStruct((rows, cin, cols), F32),
            jax.ShapeDtypeStruct((taps, chan), F32),
        ),
        in_specs=[vmem] * 5,
        out_specs=(vmem,) * 3,
        scratch_shapes=[
            pltpu.VMEM((n_pb, tgt, chan), BF16),
            pltpu.VMEM((n_pb, tgt, n_q), F32),
            pltpu.VMEM((tgt, n_q), F32),
            pltpu.VMEM((n_pb, 1, n_q), F32),
            pltpu.VMEM((n_pb, 1, n_q), F32),
            pltpu.VMEM((n_pb, 1, n_q), F32),
            pltpu.VMEM((8, n_q), F32),
            pltpu.VMEM((n_ta, 8, n_q), F32),
            pltpu.VMEM((n_pb, tgt, chan), BF16),
            pltpu.VMEM((n_pb, tgt, chan), BF16),
            pltpu.VMEM((chan, n_q), F32),
            pltpu.VMEM((n_ta, chan // n_ta, n_q), BF16),
            pltpu.VMEM((chan, n_q), BF16),
            pltpu.VMEM((2, cin, cols), BF16),
            pltpu.VMEM((3 * cin, (rows + 2) * cols), BF16),
            pltpu.VMEM((chan, n_q), BF16),
            pltpu.VMEM((2, cin, cols), F32),
            pltpu.VMEM((2, cin, cols), F32),
            pltpu.VMEM((taps, chan), F32),
            pltpu.VMEM((taps, chan), BF16),
            pltpu.VMEM((n_pb, gw_rows, chan), BF16),
            pltpu.VMEM((taps, chan), F32),
            dma((n_z,)), dma((n_z,)), dma((n_pb,)),
            dma((n_ta,)), dma((n_ta,)),
            dma((n_pb,)), dma((n_pb,)),
            dma((n_ta,)), dma((n_ta,)),
            dma((n_ta,)), dma((n_ta,)),
            dma((2,)), dma((2,)),
            dma((2,)), dma((2,)),
            dma((n_pb,)), dma((n_pb,)),
            dma((n_pb,)), dma((n_pb,)),
        ],
        compiler_params=pltpu.CompilerParams(collective_id=0, has_side_effects=True),
        name="matching",
    )(
        feat_one.reshape(n_q, chan),
        feat_two[0],
        cot_flow.reshape(2, n_q),
        enc_input,
        enc_weight.reshape(taps, chan),
    )
    return (
        outs[0][None],
        outs[1],
        outs[2].reshape(3, 3, cin, chan),
    )


def solution(mesh):
    in_specs = (
        P("pb", None, None),
        P("ta", "pb", None),
        P(None, "pb", None),
        P("pb", "ta", None),
        P(None, None, "ta", None),
    )
    out_specs = (P("ta", "pb", None), P("pb", "ta", None), P(None, None, "ta", None))
    body = functools.partial(per_device, mesh.shape["pb"], mesh.shape["ta"])
    return jax.shard_map(
        body, mesh=mesh, in_specs=in_specs, out_specs=out_specs, check_vma=False
    )
```

time: 238 us -> 47.4 us (0.20)
  waiting for transfers between devices: 138 us -> 0 us
  blocking collectives: 63.3 us -> 0 us
  Pallas kernels: 0 us -> 42.4 us
  between operations: 14.2 us -> 0.66 us
  matrix products: 6.56 us -> 0 us
  other arithmetic: 5.61 us -> 0 us
  starting transfers between devices: 4.93 us -> 0 us
    reduce_scatter x1 -> x0, waiting for transfers between devices: 67.2 us -> none  [per_device(): lax.psum_scatter(target_terms, 'pb', scatter_dimension=0, tiled=True)]
    psum x1 -> x0, waiting for transfers between devices: 66 us -> none  [per_device(): grad_weight = lax.psum(grad_weight, 'pb')]
    all_gather x4 -> x0, blocking collectives: 48.8 us -> none  [the longest x1 33.2 us: per_device(): targets = lax.all_gather(feat_two, 'pb', axis=1, tiled=True)[0]]
    pallas_call x0 -> x1, Pallas kernels: none -> 42.4 us  [per_device(): pl.pallas_call(functools.partial(kernel, n_pb, n_ta, rows, cols, gw_rows)...]
    psum x1 -> x0, blocking collectives: 14.5 us -> none  [per_device(): feat_grad = lax.psum(partial_grad, 'ta').astype(jnp.bfloat16)]
    dot_general x21 -> x0, matrix products: 6.56 us -> none  [the longest x9 2.04 us: per_device(): jnp.einsum('yxo,io->yix', shifted, enc_weight[row_off, col_off], preferre...]
    ppermute x2 -> x0, waiting for transfers between devices: 4.86 us -> none  [the longest x1 4.27 us: padded_2(): after = lax.ppermute(first, axis, down)]
    ppermute x2 -> x0, starting transfers between devices: 4.85 us -> none  [the longest x1 3.56 us: padded_2(): before = lax.ppermute(last, axis, up)]
  transfers between devices with their start and end apart: 4 -> 0, of which waited for: 4 -> 0; matrix products, arithmetic and copies ran while one was open for 2% -> 0% of each run, Pallas kernels for 0% -> 0%
where the time goes in v1:
time: 47.4 us; the launch traced here: 47.2 us
  Pallas kernels  42.4 us (89%)
  local copies, waits for them, and re-layouts  4.18 us (9%)
  between operations  0.66 us (1%)
    pallas_call x1, Pallas kernels, per_device(): pl.pallas_call(functools.partial(kernel, n_pb, n_ta, rows, cols, gw_rows)...  42.4 us
    unnamed x10, local copies, waits for them, and re-layouts  4.18 us

profile of v1, /device:TPU:0, one launch (start us, length us, event | category | flops | bytes accessed | tf_op | source)
XLA Modules:
  0.0 47.2 jit_solution(11198290018900656603)
XLA Ops:
  0.6 0.0 copy-start.2
  0.6 0.7 %copy-done.2 = f32[2,2,256]{2,1,0:T(2,128)S(1)} copy-done((f32[2,2,256]{2,1,0:T(2,128)S(1)}, f32[2,2,256]{2,1,0:T(2,128)}, u32[]{:S(2)}) %copy-start.2) | copy-done | bytes 4120
  1.3 0.6 %copy.8 = f32[1,2,2,256]{3,1,2,0:T(2,128)} copy(f32[1,2,2,256]{3,2,1,0:T(2,128)S(1)} %bitcast.13) | data formatting | bytes 8192
  1.9 42.4 %matching.1 = (f32[256,128]{1,0:T(8,128)}, f32[2,32,256]{2,1,0:T(8,128)}, f32[288,128]{1,0:T(8,128)}) custom-call(bf16[512,128]{1,0:T(8,128)(2,1)} %bitcast.8, bf16[256,128]{1,0:T(8,128)(2,1)} %bitcast.11, f32[2,512]{1,0:T(2,128)} %bitcast.12, bf16[2,32,256]{2,1,0:T(8,128)(2,1)} %in_ref.1, bf16[288,128]{1,0:T(8,128)(2,1)} %bitcast.10), custom_call_target="tpu_custom_call" | custom-call | tf_op jit(solution)/shard_map/matching/pallas_call | solution.py:413
  44.3 0.0 copy-start.1
  44.3 0.0 copy-start
  44.3 1.6 %copy.12 = f32[1,256,128]{2,1,0:T(8,128)} copy(f32[1,256,128]{2,1,0:T(8,128)} %bitcast.9) | data formatting | bytes 262144
  45.9 0.0 copy-done.1
  46.0 0.6 %copy.13 = f32[2,32,256]{2,1,0:T(8,128)} copy(f32[2,32,256]{2,1,0:T(8,128)S(1)} %copy-done.1) | data formatting | bytes 131072
  46.6 0.0 copy-done
  46.6 0.7 %copy.14 = f32[3,3,32,128]{3,2,1,0:T(8,128)} copy(f32[3,3,32,128]{3,2,1,0:T(8,128)S(1)} %bitcast.7) | data formatting | bytes 294912
Async XLA Ops:
  0.6 0.7 %copy-start.2 = (f32[2,2,256]{2,1,0:T(2,128)S(1)}, f32[2,2,256]{2,1,0:T(2,128)}, u32[]{:S(2)}) copy-start(f32[2,2,256]{2,1,0:T(2,128)} %param.7) | copy-start | bytes 12292
  44.3 1.6 %copy-start.1 = (f32[2,32,256]{2,1,0:T(8,128)S(1)}, f32[2,32,256]{2,1,0:T(8,128)}, u32[]{:S(2)}) copy-start(f32[2,32,256]{2,1,0:T(8,128)} %get-tuple-element.13) | copy-start | bytes 196612
  44.3 2.3 %copy-start = (f32[288,128]{1,0:T(8,128)S(1)}, f32[288,128]{1,0:T(8,128)}, u32[]{:S(2)}) copy-start(f32[288,128]{1,0:T(8,128)} %get-tuple-element.8) | copy-start | bytes 442372

commit v2 on v1

v2 whole, which is shorter than its diff:
```python
import functools
import math

import jax
import jax.numpy as jnp
from jax import lax
from jax.experimental import pallas as pl
from jax.experimental.pallas import tpu as pltpu
from jax.sharding import PartitionSpec as P

FRAME_COLS = 512
MESH = pl.DeviceIdType.MESH
F32 = jnp.float32
BF16 = jnp.bfloat16


def remote(src, dst, send_sem, recv_sem, where):
    return pltpu.make_async_remote_copy(
        src_ref=src,
        dst_ref=dst,
        send_sem=send_sem,
        recv_sem=recv_sem,
        device_id=where,
        device_id_type=MESH,
    )


def matmul(left, right, dims):
    return lax.dot_general(left, right, (dims, ((), ())), preferred_element_type=F32)


def moved(value, step):
    if step == 0:
        return value
    width = value.shape[1]
    lane = lax.broadcasted_iota(jnp.int32, value.shape, 1)
    rolled = pltpu.roll(value, step % width, 1)
    edge = 0 if step > 0 else width - 1
    return jnp.where(lane == edge, 0.0, rolled)


def kernel(
    n_pb, n_ta, rows, cols, gw_rows,
    q_ref, k_ref, flow_ref, in_ref, w_ref,
    g2_ref, gi_ref, gw_ref,
    q_all, flow_in, flow_all, k_all, expo, grads, iota, peaks, totals, pulls, stats, stats_in,
    finals, g_out, g_in, f_part, f_out, f_in, feat_ref, halo_in, in_sh,
    edge_out, edge_in, gw_part, gw_send, gw_in, gw_all,
    q_send, q_recv, k_send, k_recv, s_send, s_recv, g_send, g_recv,
    f_send, f_recv, a_send, a_recv, h_send, h_recv, e_send, e_recv,
    w_send, w_recv, v_send, v_recv,
):
    me = lax.axis_index("pb")
    grp = lax.axis_index("ta")
    zz, xx = me // 2, me % 2
    n_z = n_pb // 2
    other = 1 - xx
    mate = zz * 2 + other
    n_q, chan = q_ref.shape
    tgt = k_ref.shape[0]
    n_own = gw_part.shape[0] // gw_rows
    inv_scale = 1.0 / math.sqrt(chan)
    unit = inv_scale / math.log(2.0)
    team = [(dx, dt) for dx in (1, 0) for dt in range(n_ta - 1, -1, -1) if dx or dt]

    def mate_at(dx, dt):
        x, t = lax.rem(xx + dx, 2), lax.rem(grp + dt, n_ta)
        return x, t, {"pb": zz * 2 + x, "ta": t}

    def source_at(dx, dt):
        x, t = lax.rem(xx + dx, 2), lax.rem(grp + n_ta - dt, n_ta)
        return x * n_ta + t

    slot = xx * n_ta + grp

    barrier = pltpu.get_barrier_semaphore()

    def greet(d, _):
        pl.semaphore_signal(
            barrier, inc=1, device_id={"pb": lax.rem(me + d, n_pb)}, device_id_type=MESH
        )
        return 0

    lax.fori_loop(1, n_pb, greet, 0)
    for dx, dt in team:
        if dt:
            pl.semaphore_signal(
                barrier, inc=1, device_id=mate_at(dx, dt)[2], device_id_type=MESH
            )

    def spread_flow(ref, half):
        for r in range(rows):
            for comp in range(2):
                flow_all[half, comp : comp + 1, r * cols : (r + 1) * cols] = ref[
                    comp, r : r + 1, :
                ]

    def place_of(origin):
        k0 = (grp * n_pb + origin * 2 + xx) * tgt
        col0 = (lax.rem(k0, FRAME_COLS) - FRAME_COLS // 2).astype(F32)
        return col0, (k0 // FRAME_COLS).astype(F32)

    def score_block(origin, half):
        raw = matmul(k_all[origin], q_all[half], ((1,), (1,)))
        peak = jnp.max(raw, axis=0, keepdims=True) * unit
        value = jnp.exp2(raw * unit - peak)
        index = half * n_z + origin
        expo[index] = value
        col0, row = place_of(origin)
        total = jnp.sum(value, axis=0, keepdims=True)
        along = jnp.sum(value * iota[...], axis=0, keepdims=True)
        peaks[index] = peak
        totals[index] = total
        pulls[index] = flow_all[half, 0:1, :] * (along + col0 * total) + flow_all[
            half, 1:2, :
        ] * (row * total)

    k_all[zz] = k_ref[...]
    q_all[xx] = q_ref[...]
    spread_flow(flow_ref, xx)
    iota[...] = lax.broadcasted_iota(jnp.int32, (tgt, n_q), 0).astype(F32)
    score_block(zz, xx)
    pl.semaphore_wait(barrier, n_pb - 1 + 2 * (n_ta - 1))

    q_copy = remote(q_ref, q_all.at[xx], q_send.at[0], q_recv.at[0], {"pb": mate})
    flow_copy = remote(flow_ref, flow_in, q_send.at[1], q_recv.at[1], {"pb": mate})
    q_copy.start()
    flow_copy.start()

    def near(fn):
        def step(t, _):
            dist = t // 2 + 1
            z = zz + dist * (1 - 2 * (t % 2))

            @pl.when(jnp.logical_and(z >= 0, z < n_z))
            def _():
                fn(z)

            return 0

        lax.fori_loop(0, 2 * (n_z - 1), step, 0)

    def k_copy(z):
        return remote(
            k_ref, k_all.at[zz], k_send.at[z], k_recv.at[zz], {"pb": z * 2 + xx}
        )

    near(lambda z: k_copy(z).start())

    up = {"pb": lax.rem(me + 1, n_pb)}
    down = {"pb": lax.rem(me + n_pb - 1, n_pb)}
    h_up = remote(in_ref.at[rows - 1], halo_in.at[0], h_send.at[0], h_recv.at[0], up)
    h_down = remote(in_ref.at[0], halo_in.at[1], h_send.at[1], h_recv.at[1], down)
    h_up.start()
    h_down.start()

    cin = in_ref.shape[1]

    def spread_rows(value, place):
        for b in range(3):
            in_sh[b * cin : (b + 1) * cin, place * cols : (place + 1) * cols] = moved(
                value, 1 - b
            ).astype(BF16)

    for y in range(rows):
        spread_rows(in_ref[y].astype(F32), y + 1)

    flow_copy.wait_recv()
    spread_flow(flow_in, other)
    remote(q_ref, q_all.at[other], q_send.at[0], q_recv.at[0], {"pb": mate}).wait_recv()
    score_block(zz, other)

    def take(z):
        remote(
            k_all.at[z], k_all.at[z], k_send.at[z], k_recv.at[z], {"pb": z * 2 + xx}
        ).wait_recv()
        for half in range(2):
            score_block(z, half)

    near(take)

    for half in range(2):
        all_peaks = peaks[half * n_z : (half + 1) * n_z]
        peak = jnp.max(all_peaks, axis=0)
        decay = jnp.exp2(all_peaks - peak[None])
        first = 3 * half
        stats[first : first + 1, :] = peak
        stats[first + 1 : first + 2, :] = jnp.sum(
            totals[half * n_z : (half + 1) * n_z] * decay, axis=0
        )
        stats[first + 2 : first + 3, :] = jnp.sum(
            pulls[half * n_z : (half + 1) * n_z] * decay, axis=0
        )
    stat_copies = []
    for i, (dx, dt) in enumerate(team):
        stat_copies.append(
            remote(
                stats, stats_in.at[slot], s_send.at[i], s_recv.at[slot], mate_at(dx, dt)[2]
            )
        )
        stat_copies[-1].start()

    h_up.wait_recv()
    h_down.wait_recv()
    for side, place in ((0, 0), (1, rows + 1)):
        at_end = (me == 0) if side == 0 else (me == n_pb - 1)
        spread_rows(halo_in[side].astype(F32) * jnp.where(at_end, 0.0, 1.0), place)
    f_part[...] = jnp.zeros_like(f_part)

    stats_in[slot] = stats[...]
    for i, (dx, dt) in enumerate(team):
        frm = source_at(dx, dt)
        remote(
            stats, stats_in.at[frm], s_send.at[i], s_recv.at[frm], mate_at(dx, dt)[2]
        ).wait_recv()
    for half in range(2):
        first = 3 * half
        all_peaks = stats_in[:, first : first + 1, :]
        peak = jnp.max(all_peaks, axis=0)
        decay = jnp.exp2(all_peaks - peak[None])
        total = jnp.sum(stats_in[:, first + 1 : first + 2, :] * decay, axis=0)
        weighted = jnp.sum(stats_in[:, first + 2 : first + 3, :] * decay, axis=0)
        finals[half, 0:1, :] = peak
        finals[half, 1:2, :] = weighted / total
        finals[half, 2:3, :] = inv_scale / total

    part = chan // n_ta

    def rows_of(ref, index):
        return ref.at[pl.ds(pl.multiple_of(index * part, part), part), :]

    def feat_half(half):
        def step(origin, _):
            index = half * n_z + origin
            col0, row = place_of(origin)
            scale = jnp.exp2(peaks[index] - finals[half, 0:1, :]) * finals[half, 2:3, :]
            slope = flow_all[half, 0:1, :]
            rest = col0 * slope + row * flow_all[half, 1:2, :] - finals[half, 1:2, :]
            grad = (expo[index] * scale * (iota[...] * slope + rest)).astype(BF16)
            grads[index] = grad
            f_part[half] += matmul(k_all[origin], grad, ((0,), (0,)))
            return 0

        lax.fori_loop(0, n_z, step, 0)
        f_out[half] = f_part[half].astype(BF16)

    f_copies = []

    def send_half(half, dx):
        for i, (ox, dt) in enumerate(team):
            if ox == dx:
                _, t, where = mate_at(ox, dt)
                f_copies.append(
                    remote(
                        rows_of(f_out.at[half], t), f_in.at[slot], f_send.at[i],
                        f_recv.at[slot], where,
                    )
                )
                f_copies[-1].start()

    feat_half(other)
    send_half(other, 1)
    feat_half(xx)
    send_half(xx, 0)

    def target_terms(origin):
        return matmul(grads[origin], q_all[0], ((1,), (0,))) + matmul(
            grads[n_z + origin], q_all[1], ((1,), (0,))
        )

    def g_copy(z):
        return remote(
            g_out.at[z], g_in.at[zz], g_send.at[z], g_recv.at[zz], {"pb": z * 2 + xx}
        )

    def g_step(z):
        g_out[z] = target_terms(z).astype(BF16)
        g_copy(z).start()

    near(g_step)
    g2_ref[...] = target_terms(zz)

    total_f = f_part[xx, pl.ds(pl.multiple_of(grp * part, part), part), :]
    for i, (dx, dt) in enumerate(team):
        frm = source_at(dx, dt)
        remote(
            f_in.at[frm], f_in.at[frm], f_send.at[i], f_recv.at[frm], mate_at(dx, dt)[2]
        ).wait_recv()
        total_f = total_f + f_in[frm].astype(F32)
    feat_ref[pl.ds(pl.multiple_of(grp * part, part), part), :] = total_f.astype(BF16)
    a_copies = []
    for d in range(1, n_ta):
        to = lax.rem(grp + d, n_ta)
        a_copies.append(
            remote(
                rows_of(feat_ref, grp), rows_of(feat_ref, grp), a_send.at[d], a_recv.at[grp],
                {"ta": to},
            )
        )
        a_copies[-1].start()
    for d in range(1, n_ta):
        frm = lax.rem(grp + n_ta - d, n_ta)
        remote(
            rows_of(feat_ref, frm), rows_of(feat_ref, frm), a_send.at[d], a_recv.at[frm],
            {"ta": frm},
        ).wait_recv()

    feat = feat_ref[...]
    width = 3 * cin
    for a in range(3):
        gw_part[a * width : (a + 1) * width, :] = matmul(
            in_sh[:, a * cols : (a + rows) * cols], feat, ((1,), (1,))
        )
    gw_send[...] = gw_part[...].astype(BF16)

    def gw_chunk(ref, index):
        return ref.at[pl.ds(pl.multiple_of(index * gw_rows, gw_rows), gw_rows), :]

    def w_copy(d):
        to = lax.rem(me + d, n_pb)
        return to, remote(
            gw_chunk(gw_send, to), gw_in.at[me], w_send.at[d], w_recv.at[me], {"pb": to}
        )

    def w_start(d, _):
        to = lax.rem(me + d, n_pb)

        @pl.when(to < n_own)
        def _():
            w_copy(d)[1].start()

        return 0

    lax.fori_loop(1, n_pb, w_start, 0)

    spread = matmul(w_ref[...], feat, ((1,), (0,)))
    outs = [None] * (rows + 2)
    for r in range(rows):
        for a in range(3):
            term = None
            for b in range(3):
                first = (a * 3 + b) * cin
                piece = moved(
                    spread[first : first + cin, r * cols : (r + 1) * cols], b - 1
                )
                term = piece if term is None else term + piece
            place = r + a
            outs[place] = term if outs[place] is None else outs[place] + term
    edge_out[0] = outs[rows + 1]
    edge_out[1] = outs[0]
    e_up = remote(edge_out.at[0], edge_in.at[0], e_send.at[0], e_recv.at[0], up)
    e_down = remote(edge_out.at[1], edge_in.at[1], e_send.at[1], e_recv.at[1], down)
    e_up.start()
    e_down.start()
    for y in range(rows):
        gi_ref[y] = outs[y + 1]

    @pl.when(me < n_own)
    def _():
        first = pl.multiple_of(me * gw_rows, gw_rows)
        gw_all[pl.ds(first, gw_rows), :] = gw_part[pl.ds(first, gw_rows), :]

        def add(d, _):
            frm = lax.rem(me + n_pb - d, n_pb)
            remote(
                gw_in.at[frm], gw_in.at[frm], w_send.at[d], w_recv.at[frm], {"pb": frm}
            ).wait_recv()
            gw_all[pl.ds(first, gw_rows), :] += gw_in[frm].astype(F32)
            return 0

        lax.fori_loop(1, n_pb, add, 0)

        def give(d, _):
            to = lax.rem(me + d, n_pb)
            remote(
                gw_chunk(gw_all, me), gw_chunk(gw_all, me), v_send.at[d], v_recv.at[me],
                {"pb": to},
            ).start()
            return 0

        lax.fori_loop(1, n_pb, give, 0)

    def g_add(z):
        remote(
            g_in.at[z], g_in.at[z], g_send.at[z], g_recv.at[z], {"pb": z * 2 + xx}
        ).wait_recv()
        g2_ref[...] += g_in[z].astype(F32)

    near(g_add)

    e_up.wait_recv()
    e_down.wait_recv()
    gi_ref[0] += edge_in[0] * jnp.where(me == 0, 0.0, 1.0)
    gi_ref[rows - 1] += edge_in[1] * jnp.where(me == n_pb - 1, 0.0, 1.0)

    def v_wait(d, _):
        frm = lax.rem(me + n_pb - d, n_pb)

        @pl.when(frm < n_own)
        def _():
            remote(
                gw_chunk(gw_all, frm), gw_chunk(gw_all, frm), v_send.at[d], v_recv.at[frm],
                {"pb": frm},
            ).wait_recv()

        return 0

    lax.fori_loop(1, n_pb, v_wait, 0)
    gw_ref[...] = gw_all[...]

    for copy in (
        q_copy, flow_copy, h_up, h_down, e_up, e_down, *stat_copies, *f_copies, *a_copies
    ):
        copy.wait_send()

    def gone(z):
        k_copy(z).wait_send()
        g_copy(z).wait_send()

    near(gone)

    def drain(d, _):
        @pl.when(lax.rem(me + d, n_pb) < n_own)
        def _():
            w_copy(d)[1].wait_send()

        @pl.when(me < n_own)
        def _():
            remote(
                gw_chunk(gw_all, me), gw_chunk(gw_all, me), v_send.at[d], v_recv.at[me],
                {"pb": lax.rem(me + d, n_pb)},
            ).wait_send()

        return 0

    lax.fori_loop(1, n_pb, drain, 0)


def per_device(n_pb, n_ta, feat_one, feat_two, cot_flow, enc_input, enc_weight):
    rows, cols, chan = feat_one.shape
    n_q = rows * cols
    tgt = feat_two.shape[1]
    cin = enc_input.shape[1]
    taps = 9 * cin
    assert n_pb % 2 == 0 and FRAME_COLS % tgt == 0 and taps % 16 == 0
    gw_rows = 16 * pl.cdiv(taps // 16, n_pb)
    assert taps % gw_rows == 0
    vmem = pl.BlockSpec(memory_space=pltpu.VMEM)
    dma = pltpu.SemaphoreType.DMA
    n_z = n_pb // 2
    outs = pl.pallas_call(
        functools.partial(kernel, n_pb, n_ta, rows, cols, gw_rows),
        out_shape=(
            jax.ShapeDtypeStruct((tgt, chan), F32),
            jax.ShapeDtypeStruct((rows, cin, cols), F32),
            jax.ShapeDtypeStruct((taps, chan), F32),
        ),
        in_specs=[vmem] * 5,
        out_specs=(vmem,) * 3,
        scratch_shapes=[
            pltpu.VMEM((2, n_q, chan), BF16),
            pltpu.VMEM((2, rows, cols), F32),
            pltpu.VMEM((2, 8, n_q), F32),
            pltpu.VMEM((n_z, tgt, chan), BF16),
            pltpu.VMEM((n_pb, tgt, n_q), F32),
            pltpu.VMEM((n_pb, tgt, n_q), BF16),
            pltpu.VMEM((tgt, n_q), F32),
            pltpu.VMEM((n_pb, 1, n_q), F32),
            pltpu.VMEM((n_pb, 1, n_q), F32),
            pltpu.VMEM((n_pb, 1, n_q), F32),
            pltpu.VMEM((8, n_q), F32),
            pltpu.VMEM((2 * n_ta, 8, n_q), F32),
            pltpu.VMEM((2, 8, n_q), F32),
            pltpu.VMEM((n_z, tgt, chan), BF16),
            pltpu.VMEM((n_z, tgt, chan), BF16),
            pltpu.VMEM((2, chan, n_q), F32),
            pltpu.VMEM((2, chan, n_q), BF16),
            pltpu.VMEM((2 * n_ta, chan // n_ta, n_q), BF16),
            pltpu.VMEM((chan, n_q), BF16),
            pltpu.VMEM((2, cin, cols), BF16),
            pltpu.VMEM((3 * cin, (rows + 2) * cols), BF16),
            pltpu.VMEM((2, cin, cols), F32),
            pltpu.VMEM((2, cin, cols), F32),
            pltpu.VMEM((taps, chan), F32),
            pltpu.VMEM((taps, chan), BF16),
            pltpu.VMEM((n_pb, gw_rows, chan), BF16),
            pltpu.VMEM((taps, chan), F32),
            dma((2,)), dma((2,)),
            dma((n_z,)), dma((n_z,)),
            dma((2 * n_ta,)), dma((2 * n_ta,)),
            dma((n_z,)), dma((n_z,)),
            dma((2 * n_ta,)), dma((2 * n_ta,)),
            dma((n_ta,)), dma((n_ta,)),
            dma((2,)), dma((2,)),
            dma((2,)), dma((2,)),
            dma((n_pb,)), dma((n_pb,)),
            dma((n_pb,)), dma((n_pb,)),
        ],
        compiler_params=pltpu.CompilerParams(collective_id=0, has_side_effects=True),
        name="matching",
    )(
        feat_one.reshape(n_q, chan),
        feat_two[0],
        cot_flow,
        enc_input,
        enc_weight.reshape(taps, chan),
    )
    return (
        outs[0][None],
        outs[1],
        outs[2].reshape(3, 3, cin, chan),
    )


def solution(mesh):
    in_specs = (
        P("pb", None, None),
        P("ta", "pb", None),
        P(None, "pb", None),
        P("pb", "ta", None),
        P(None, None, "ta", None),
    )
    out_specs = (P("ta", "pb", None), P("pb", "ta", None), P(None, None, "ta", None))
    body = functools.partial(per_device, mesh.shape["pb"], mesh.shape["ta"])
    return jax.shard_map(
        body, mesh=mesh, in_specs=in_specs, out_specs=out_specs, check_vma=False
    )
```

time: 47.4 us -> 42.9 us (0.905)
  Pallas kernels: 42.4 us -> 39.2 us
  local copies, waits for them, and re-layouts: 4.18 us -> 2.91 us
    pallas_call x1, Pallas kernels: 42.4 us -> 39.2 us  [per_device(): pl.pallas_call(functools.partial(kernel, n_pb, n_ta, rows, cols, gw_rows)...]
    unnamed x10 -> x7, local copies, waits for them, and re-layouts: 4.18 us -> 2.91 us
where the time goes in v2:
time: 42.9 us; the launch traced here: 42.8 us
  Pallas kernels  39.2 us (91%)
  local copies, waits for them, and re-layouts  2.91 us (7%)
  between operations  0.66 us (2%)
    pallas_call x1, Pallas kernels, per_device(): pl.pallas_call(functools.partial(kernel, n_pb, n_ta, rows, cols, gw_rows)...  39.2 us
    unnamed x7, local copies, waits for them, and re-layouts  2.91 us

profile of v2, /device:TPU:0, one launch (start us, length us, event | category | flops | bytes accessed | tf_op | source)
XLA Modules:
  0.0 42.8 jit_solution(13779938572532320280)
XLA Ops:
  0.6 39.2 %matching.1 = (f32[256,128]{1,0:T(8,128)}, f32[2,32,256]{2,1,0:T(8,128)}, f32[288,128]{1,0:T(8,128)}) custom-call(bf16[512,128]{1,0:T(8,128)(2,1)} %bitcast.6, bf16[256,128]{1,0:T(8,128)(2,1)} %bitcast.9, f32[2,2,256]{2,1,0:T(2,128)} %flow_ref.1, bf16[2,32,256]{2,1,0:T(8,128)(2,1)} %in_ref.1, bf16[288,128]{1,0:T(8,128)(2,1)} %bitcast.8), custom_call_target="tpu_custom_call" | custom-call | tf_op jit(solution)/shard_map/matching/pallas_call | solution.py:451
  39.8 0.0 copy-start.1
  39.8 0.0 copy-start
  39.9 1.6 %copy.11 = f32[1,256,128]{2,1,0:T(8,128)} copy(f32[1,256,128]{2,1,0:T(8,128)} %bitcast.7) | data formatting | bytes 262144
  41.5 0.0 copy-done.1
  41.5 0.6 %copy.12 = f32[2,32,256]{2,1,0:T(8,128)} copy(f32[2,32,256]{2,1,0:T(8,128)S(1)} %copy-done.1) | data formatting | bytes 131072
  42.1 0.0 copy-done
  42.1 0.7 %copy.13 = f32[3,3,32,128]{3,2,1,0:T(8,128)} copy(f32[3,3,32,128]{3,2,1,0:T(8,128)S(1)} %bitcast.5) | data formatting | bytes 294912
Async XLA Ops:
  39.8 1.6 %copy-start.1 = (f32[2,32,256]{2,1,0:T(8,128)S(1)}, f32[2,32,256]{2,1,0:T(8,128)}, u32[]{:S(2)}) copy-start(f32[2,32,256]{2,1,0:T(8,128)} %get-tuple-element.13) | copy-start | bytes 196612
  39.8 2.3 %copy-start = (f32[288,128]{1,0:T(8,128)S(1)}, f32[288,128]{1,0:T(8,128)}, u32[]{:S(2)}) copy-start(f32[288,128]{1,0:T(8,128)} %get-tuple-element.8) | copy-start | bytes 442372

commit v3 on v2

--- a/solution.py
+++ b/solution.py
@@ -41,11 +41,11 @@
 
 def kernel(
     n_pb, n_ta, rows, cols, gw_rows,
-    q_ref, k_ref, flow_ref, in_ref, w_ref,
+    q_hbm, k_hbm, flow_hbm, in_hbm, w_hbm,
     g2_ref, gi_ref, gw_ref,
-    q_all, flow_in, flow_all, k_all, expo, grads, iota, peaks, totals, pulls, stats, stats_in,
+    flow_ref, in_ref, w_ref, load_sem, q_all, flow_in, flow_all, k_all, expo, grads, iota, peaks, totals, pulls, stats, stats_in,
     finals, g_out, g_in, f_part, f_out, f_in, feat_ref, halo_in, in_sh,
-    edge_out, edge_in, gw_part, gw_send, gw_in, gw_all,
+    edge_out, edge_in, gw_part, gw_send, gw_in, gw_sum, gw_all,
     q_send, q_recv, k_send, k_recv, s_send, s_recv, g_send, g_recv,
     f_send, f_recv, a_send, a_recv, h_send, h_recv, e_send, e_recv,
     w_send, w_recv, v_send, v_recv,
@@ -56,9 +56,17 @@
     n_z = n_pb // 2
     other = 1 - xx
     mate = zz * 2 + other
-    n_q, chan = q_ref.shape
-    tgt = k_ref.shape[0]
-    n_own = gw_part.shape[0] // gw_rows
+    n_q, chan = q_hbm.shape
+    tgt = k_hbm.shape[0]
+    n_own = n_pb // 2
+    own_first = n_pb // 4
+    own = me - own_first
+    is_own = jnp.logical_and(own >= 0, own < n_own)
+
+    def gw_start(index):
+        last = gw_part.shape[0] - gw_rows
+        return pl.multiple_of(index * last // (n_own - 1) // 16 * 16, 16)
+
     inv_scale = 1.0 / math.sqrt(chan)
     unit = inv_scale / math.log(2.0)
     team = [(dx, dt) for dx in (1, 0) for dt in range(n_ta - 1, -1, -1) if dx or dt]
@@ -87,6 +95,19 @@
             pl.semaphore_signal(
                 barrier, inc=1, device_id=mate_at(dx, dt)[2], device_id_type=MESH
             )
+
+    q_ref, k_ref = q_all.at[xx], k_all.at[zz]
+    loads = [
+        pltpu.make_async_copy(src, dst, load_sem.at[i])
+        for i, (src, dst) in enumerate(
+            (
+                (k_hbm, k_ref), (q_hbm, q_ref), (flow_hbm, flow_ref), (in_hbm, in_ref),
+                (w_hbm, w_ref),
+            )
+        )
+    ]
+    for load in loads:
+        load.start()
 
     def spread_flow(ref, half):
         for r in range(rows):
@@ -115,10 +136,10 @@
             half, 1:2, :
         ] * (row * total)
 
-    k_all[zz] = k_ref[...]
-    q_all[xx] = q_ref[...]
+    iota[...] = lax.broadcasted_iota(jnp.int32, (tgt, n_q), 0).astype(F32)
+    for load in loads:
+        load.wait()
     spread_flow(flow_ref, xx)
-    iota[...] = lax.broadcasted_iota(jnp.int32, (tgt, n_q), 0).astype(F32)
     score_block(zz, xx)
     pl.semaphore_wait(barrier, n_pb - 1 + 2 * (n_ta - 1))
 
@@ -167,7 +188,7 @@
 
     flow_copy.wait_recv()
     spread_flow(flow_in, other)
-    remote(q_ref, q_all.at[other], q_send.at[0], q_recv.at[0], {"pb": mate}).wait_recv()
+    remote(q_all.at[other], q_all.at[other], q_send.at[0], q_recv.at[0], {"pb": mate}).wait_recv()
     score_block(zz, other)
 
     def take(z):
@@ -313,25 +334,23 @@
         )
     gw_send[...] = gw_part[...].astype(BF16)
 
-    def gw_chunk(ref, index):
-        return ref.at[pl.ds(pl.multiple_of(index * gw_rows, gw_rows), gw_rows), :]
-
-    def w_copy(d):
-        to = lax.rem(me + d, n_pb)
-        return to, remote(
-            gw_chunk(gw_send, to), gw_in.at[me], w_send.at[d], w_recv.at[me], {"pb": to}
-        )
-
-    def w_start(d, _):
-        to = lax.rem(me + d, n_pb)
-
-        @pl.when(to < n_own)
-        def _():
-            w_copy(d)[1].start()
-
-        return 0
-
-    lax.fori_loop(1, n_pb, w_start, 0)
+    def w_copy(index):
+        return remote(
+            gw_send.at[pl.ds(gw_start(index), gw_rows), :], gw_in.at[me],
+            w_send.at[index], w_recv.at[me], {"pb": own_first + index},
+        )
+
+    def to_owners(fn):
+        def step(index, _):
+            @pl.when(index != own)
+            def _():
+                fn(index)
+
+            return 0
+
+        lax.fori_loop(0, n_own, step, 0)
+
+    to_owners(lambda index: w_copy(index).start())
 
     spread = matmul(w_ref[...], feat, ((1,), (0,)))
     outs = [None] * (rows + 2)
@@ -355,30 +374,30 @@
     for y in range(rows):
         gi_ref[y] = outs[y + 1]
 
-    @pl.when(me < n_own)
+    def v_copy(d):
+        return remote(
+            gw_sum, gw_all.at[own], v_send.at[d], v_recv.at[own],
+            {"pb": lax.rem(me + d, n_pb)},
+        )
+
+    @pl.when(is_own)
     def _():
-        first = pl.multiple_of(me * gw_rows, gw_rows)
-        gw_all[pl.ds(first, gw_rows), :] = gw_part[pl.ds(first, gw_rows), :]
-
-        def add(d, _):
+        def add(d, total):
             frm = lax.rem(me + n_pb - d, n_pb)
             remote(
-                gw_in.at[frm], gw_in.at[frm], w_send.at[d], w_recv.at[frm], {"pb": frm}
+                gw_in.at[frm], gw_in.at[frm], w_send.at[0], w_recv.at[frm], {"pb": frm}
             ).wait_recv()
-            gw_all[pl.ds(first, gw_rows), :] += gw_in[frm].astype(F32)
+            return total + gw_in[frm].astype(F32)
+
+        total = lax.fori_loop(1, n_pb, add, gw_part[pl.ds(gw_start(own), gw_rows), :])
+        gw_sum[...] = total.astype(BF16)
+
+        def give(d, _):
+            v_copy(d).start()
             return 0
 
-        lax.fori_loop(1, n_pb, add, 0)
-
-        def give(d, _):
-            to = lax.rem(me + d, n_pb)
-            remote(
-                gw_chunk(gw_all, me), gw_chunk(gw_all, me), v_send.at[d], v_recv.at[me],
-                {"pb": to},
-            ).start()
-            return 0
-
         lax.fori_loop(1, n_pb, give, 0)
+        gw_all[own] = gw_sum[...]
 
     def g_add(z):
         remote(
@@ -393,20 +412,19 @@
     gi_ref[0] += edge_in[0] * jnp.where(me == 0, 0.0, 1.0)
     gi_ref[rows - 1] += edge_in[1] * jnp.where(me == n_pb - 1, 0.0, 1.0)
 
-    def v_wait(d, _):
-        frm = lax.rem(me + n_pb - d, n_pb)
-
-        @pl.when(frm < n_own)
-        def _():
-            remote(
-                gw_chunk(gw_all, frm), gw_chunk(gw_all, frm), v_send.at[d], v_recv.at[frm],
-                {"pb": frm},
-            ).wait_recv()
-
+    def v_wait(index):
+        remote(
+            gw_all.at[index], gw_all.at[index], v_send.at[0], v_recv.at[index],
+            {"pb": own_first + index},
+        ).wait_recv()
+
+    to_owners(v_wait)
+
+    def write(index, _):
+        gw_ref[pl.ds(gw_start(index), gw_rows), :] = gw_all[index].astype(F32)
         return 0
 
-    lax.fori_loop(1, n_pb, v_wait, 0)
-    gw_ref[...] = gw_all[...]
+    lax.fori_loop(0, n_own, write, 0)
 
     for copy in (
         q_copy, flow_copy, h_up, h_down, e_up, e_down, *stat_copies, *f_copies, *a_copies
@@ -419,21 +437,28 @@
 
     near(gone)
 
-    def drain(d, _):
-        @pl.when(lax.rem(me + d, n_pb) < n_own)
-        def _():
-            w_copy(d)[1].wait_send()
-
-        @pl.when(me < n_own)
-        def _():
-            remote(
-                gw_chunk(gw_all, me), gw_chunk(gw_all, me), v_send.at[d], v_recv.at[me],
-                {"pb": lax.rem(me + d, n_pb)},
-            ).wait_send()
-
-        return 0
-
-    lax.fori_loop(1, n_pb, drain, 0)
+    to_owners(lambda index: w_copy(index).wait_send())
+
+    @pl.when(is_own)
+    def _():
+        def drain(d, _):
+            v_copy(d).wait_send()
+            return 0
+
+        lax.fori_loop(1, n_pb, drain, 0)
+
+
+def place(g2_in, gi_in, gw_in, g2_ref, gi_ref, gw_ref, sem):
+    copies = [
+        pltpu.make_async_copy(src, dst, sem.at[i])
+        for i, (src, dst) in enumerate(
+            ((g2_in, g2_ref), (gi_in, gi_ref), (gw_in, gw_ref))
+        )
+    ]
+    for copy in copies:
+        copy.start()
+    for copy in copies:
+        copy.wait()
 
 
 def per_device(n_pb, n_ta, feat_one, feat_two, cot_flow, enc_input, enc_weight):
@@ -442,22 +467,22 @@
     tgt = feat_two.shape[1]
     cin = enc_input.shape[1]
     taps = 9 * cin
-    assert n_pb % 2 == 0 and FRAME_COLS % tgt == 0 and taps % 16 == 0
-    gw_rows = 16 * pl.cdiv(taps // 16, n_pb)
-    assert taps % gw_rows == 0
+    assert n_pb % 4 == 0 and FRAME_COLS % tgt == 0 and taps % 16 == 0
+    gw_rows = 16 * pl.cdiv(taps // 16, n_pb // 2)
     vmem = pl.BlockSpec(memory_space=pltpu.VMEM)
     dma = pltpu.SemaphoreType.DMA
     n_z = n_pb // 2
+    shapes = ((tgt, chan), (rows, cin, cols), (taps, chan))
     outs = pl.pallas_call(
         functools.partial(kernel, n_pb, n_ta, rows, cols, gw_rows),
-        out_shape=(
-            jax.ShapeDtypeStruct((tgt, chan), F32),
-            jax.ShapeDtypeStruct((rows, cin, cols), F32),
-            jax.ShapeDtypeStruct((taps, chan), F32),
-        ),
-        in_specs=[vmem] * 5,
+        out_shape=tuple(pltpu.VMEM(shape, F32) for shape in shapes),
+        in_specs=[pl.BlockSpec(memory_space=pl.ANY)] * 5,
         out_specs=(vmem,) * 3,
         scratch_shapes=[
+            pltpu.VMEM((2, rows, cols), F32),
+            pltpu.VMEM((rows, cin, cols), BF16),
+            pltpu.VMEM((taps, chan), BF16),
+            dma((5,)),
             pltpu.VMEM((2, n_q, chan), BF16),
             pltpu.VMEM((2, rows, cols), F32),
             pltpu.VMEM((2, 8, n_q), F32),
@@ -484,7 +509,8 @@
             pltpu.VMEM((taps, chan), F32),
             pltpu.VMEM((taps, chan), BF16),
             pltpu.VMEM((n_pb, gw_rows, chan), BF16),
-            pltpu.VMEM((taps, chan), F32),
+            pltpu.VMEM((gw_rows, chan), BF16),
+            pltpu.VMEM((n_pb // 2, gw_rows, chan), BF16),
             dma((2,)), dma((2,)),
             dma((n_z,)), dma((n_z,)),
             dma((2 * n_ta,)), dma((2 * n_ta,)),
@@ -493,8 +519,8 @@
             dma((n_ta,)), dma((n_ta,)),
             dma((2,)), dma((2,)),
             dma((2,)), dma((2,)),
-            dma((n_pb,)), dma((n_pb,)),
-            dma((n_pb,)), dma((n_pb,)),
+            dma((n_pb // 2,)), dma((n_pb,)),
+            dma((n_pb,)), dma((n_pb // 2,)),
         ],
         compiler_params=pltpu.CompilerParams(collective_id=0, has_side_effects=True),
         name="matching",
@@ -505,6 +531,14 @@
         enc_input,
         enc_weight.reshape(taps, chan),
     )
+    outs = pl.pallas_call(
+        place,
+        out_shape=tuple(jax.ShapeDtypeStruct(shape, F32) for shape in shapes),
+        in_specs=[vmem] * 3,
+        out_specs=(pl.BlockSpec(memory_space=pl.ANY),) * 3,
+        scratch_shapes=[dma((3,))],
+        name="place",
+    )(*(pltpu.with_memory_space_constraint(out, pltpu.VMEM) for out in outs))
     return (
         outs[0][None],
         outs[1],

time: 42.9 us -> 39.4 us (0.918)
  local copies, waits for them, and re-layouts: 2.91 us -> 0 us
  Pallas kernels: 39.2 us -> 38.6 us
    unnamed x7 -> x0, local copies, waits for them, and re-layouts: 2.91 us -> none
    pallas_call x1, Pallas kernels: 39.2 us -> 37.9 us  [per_device(): pl.pallas_call(functools.partial(kernel, n_pb, n_ta, rows, cols, gw_rows)...]
    pallas_call x0 -> x1, Pallas kernels: none -> 0.75 us  [per_device(): pl.pallas_call(place, out_shape=tuple((jax.ShapeDtypeStruct(shape, F32) f...]
where the time goes in v3:
time: 39.4 us; the launch traced here: 39.3 us
  Pallas kernels  38.6 us (98%)
  between operations  0.64 us (2%)
    pallas_call x1, Pallas kernels, per_device(): pl.pallas_call(functools.partial(kernel, n_pb, n_ta, rows, cols, gw_rows)...  37.9 us

profile of v3, /device:TPU:0, one launch (start us, length us, event | category | flops | bytes accessed | tf_op | source)
XLA Modules:
  0.0 39.3 jit_solution(5456162188724226340)
XLA Ops:
  0.6 37.9 %matching.1 = (f32[256,128]{1,0:T(8,128)S(1)}, f32[2,32,256]{2,1,0:T(8,128)S(1)}, f32[288,128]{1,0:T(8,128)S(1)}) custom-call(bf16[512,128]{1,0:T(8,128)(2,1)} %bitcast.5, bf16[256,128]{1,0:T(8,128)(2,1)} %bitcast.7, f32[2,2,256]{2,1,0:T(2,128)} %flow_hbm.1, bf16[2,32,256]{2,1,0:T(8,128)(2,1)} %in_hbm.1, bf16[288,128]{1,0:T(8,128)(2,1)} %bitcast.6), custom_call_target="tpu_custom_call" | custom-call | tf_op jit(solution)/shard_map/matching/pallas_call | solution.py:476
  38.5 0.8 %place.1 = (f32[256,128]{1,0:T(8,128)}, f32[2,32,256]{2,1,0:T(8,128)}, f32[288,128]{1,0:T(8,128)}) custom-call(f32[256,128]{1,0:T(8,128)S(1)} %get-tuple-element.9.g2_in, f32[2,32,256]{2,1,0:T(8,128)S(1)} %get-tuple-element.10.gi_in, f32[288,128]{1,0:T(8,128)S(1)} %get-tuple-element.11.gw_in), custom_call_target="tpu_custom_call" | custom-call | tf_op jit(solution)/shard_map/place/pallas_call | solution.py:534

commit v4 on v3

--- a/solution.py
+++ b/solution.py
@@ -365,8 +365,8 @@
                 term = piece if term is None else term + piece
             place = r + a
             outs[place] = term if outs[place] is None else outs[place] + term
-    edge_out[0] = outs[rows + 1]
-    edge_out[1] = outs[0]
+    edge_out[0] = outs[rows + 1].astype(BF16)
+    edge_out[1] = outs[0].astype(BF16)
     e_up = remote(edge_out.at[0], edge_in.at[0], e_send.at[0], e_recv.at[0], up)
     e_down = remote(edge_out.at[1], edge_in.at[1], e_send.at[1], e_recv.at[1], down)
     e_up.start()
@@ -409,8 +409,8 @@
 
     e_up.wait_recv()
     e_down.wait_recv()
-    gi_ref[0] += edge_in[0] * jnp.where(me == 0, 0.0, 1.0)
-    gi_ref[rows - 1] += edge_in[1] * jnp.where(me == n_pb - 1, 0.0, 1.0)
+    gi_ref[0] += edge_in[0].astype(F32) * jnp.where(me == 0, 0.0, 1.0)
+    gi_ref[rows - 1] += edge_in[1].astype(F32) * jnp.where(me == n_pb - 1, 0.0, 1.0)
 
     def v_wait(index):
         remote(
@@ -504,8 +504,8 @@
             pltpu.VMEM((chan, n_q), BF16),
             pltpu.VMEM((2, cin, cols), BF16),
             pltpu.VMEM((3 * cin, (rows + 2) * cols), BF16),
-            pltpu.VMEM((2, cin, cols), F32),
-            pltpu.VMEM((2, cin, cols), F32),
+            pltpu.VMEM((2, cin, cols), BF16),
+            pltpu.VMEM((2, cin, cols), BF16),
             pltpu.VMEM((taps, chan), F32),
             pltpu.VMEM((taps, chan), BF16),
             pltpu.VMEM((n_pb, gw_rows, chan), BF16),

time: 39.4 us -> 39.2 us (level)
  no operation moved by 1% of the time
where the time goes in v4:
time: 39.2 us; the launch traced here: 39 us
  Pallas kernels  38.4 us (98%)
  between operations  0.64 us (2%)
    pallas_call x1, Pallas kernels, per_device(): pl.pallas_call(functools.partial(kernel, n_pb, n_ta, rows, cols, gw_rows)...  37.7 us

profile of v4, /device:TPU:0, one launch (start us, length us, event | category | flops | bytes accessed | tf_op | source)
XLA Modules:
  0.0 39.0 jit_solution(5966702115724879777)
XLA Ops:
  0.6 37.7 %matching.1 = (f32[256,128]{1,0:T(8,128)S(1)}, f32[2,32,256]{2,1,0:T(8,128)S(1)}, f32[288,128]{1,0:T(8,128)S(1)}) custom-call(bf16[512,128]{1,0:T(8,128)(2,1)} %bitcast.5, bf16[256,128]{1,0:T(8,128)(2,1)} %bitcast.7, f32[2,2,256]{2,1,0:T(2,128)} %flow_hbm.1, bf16[2,32,256]{2,1,0:T(8,128)(2,1)} %in_hbm.1, bf16[288,128]{1,0:T(8,128)(2,1)} %bitcast.6), custom_call_target="tpu_custom_call" | custom-call | tf_op jit(solution)/shard_map/matching/pallas_call | solution.py:476
  38.3 0.8 %place.1 = (f32[256,128]{1,0:T(8,128)}, f32[2,32,256]{2,1,0:T(8,128)}, f32[288,128]{1,0:T(8,128)}) custom-call(f32[256,128]{1,0:T(8,128)S(1)} %get-tuple-element.9.g2_in, f32[2,32,256]{2,1,0:T(8,128)S(1)} %get-tuple-element.10.gi_in, f32[288,128]{1,0:T(8,128)S(1)} %get-tuple-element.11.gw_in), custom_call_target="tpu_custom_call" | custom-call | tf_op jit(solution)/shard_map/place/pallas_call | solution.py:534
